TPU v7x, 32 devices: a whole 2x2x4 slice. The times are simulated.
32 devices in a mesh: shot: 4 (over x, core), slab: 8 (over z, y).
Axes of the slice: x: 2, y: 2, z: 4, core: 2. Of those that a mesh axis runs over, the one named last changes fastest.
Arguments:
- fwd_prev: float32 [4, 256, 128, 128], P('shot', None, 'slab'), may hold values from -6 to 6
- fwd_now: float32 [4, 256, 128, 128], P('shot', None, 'slab'), may hold values from -6 to 6
- adj_late: float32 [4, 256, 128, 128], P('shot', None, 'slab'), may hold values from -6 to 6
- adj_last: float32 [4, 256, 128, 128], P('shot', None, 'slab'), may hold values from -6 to 6
- speed_model: float32 [512, 128, 128], P('shot', 'slab'), may hold values from 0.04 to 0.24
- anchors: int32 [4], replicated, may hold values from 0 to 256
- traces: float32 [8, 1024], P(None, ('shot', 'slab')), may hold values from -6 to 6
- dest: int32 [1024, 1], P(('shot', 'slab')), may hold values from 0 to 31; in each aligned block of 32 rows (0 to 31, 32 to 63, ...) at most 2 rows name the same one
- rec_pos: int32 [1024], P(('shot', 'slab')), may hold values from 0 to 4095
Outputs:
- image: float32 [512, 128, 128], P('shot', 'slab')
Inputs may be any that keep to these rules, and one draw needn't show every extreme that they name: `dest`: within the rows of one device (aligned blocks of 32 receivers) no value occurs more than 2 times, and some value occurs exactly 2 times.
All inputs are finite; a program needn't handle non-finite values.
Results may differ from a plain program's by a relative error of at most 0.00002.
Values sent between devices are 32-bit elements; how exact they have to be, the bound alone decides.
A program may use at most 192 MiB of HBM per device.

v0:
```python
import jax
import jax.numpy as jnp
from jax import lax
from jax.sharding import PartitionSpec as P

NSTEP = 8
CAP = 2
RDEPTH = 3


centre_coef = -2.5
near_coef = 4.0 / 3.0
far_coef = -1.0 / 12.0


def extended_2(cells, sides, width):
    for axis, dim in sides:
        count = lax.axis_size(axis)
        ends = count - 1
        head = lax.slice_in_dim(cells, 0, width, axis=dim)
        tail = lax.slice_in_dim(cells, cells.shape[dim] - width, cells.shape[dim], axis=dim)
        cells = jnp.concatenate(
            [
                lax.ppermute(tail, axis, [(i, (i + 1) % count) for i in range(ends)]),
                cells,
                lax.ppermute(head, axis, [((i + 1) % count, i) for i in range(ends)]),
            ],
            axis=dim,
        )
    return cells


def laplace(field):
    padded = jnp.pad(field, ((2, 2), (0, 0), (2, 2)))
    core = padded[2:-2, 2:-2, 2:-2]
    near = padded[1:-3, 2:-2, 2:-2] + padded[3:-1, 2:-2, 2:-2]
    near = near + padded[2:-2, 1:-3, 2:-2] + padded[2:-2, 3:-1, 2:-2]
    near = near + padded[2:-2, 2:-2, 1:-3] + padded[2:-2, 2:-2, 3:-1]
    far = padded[:-4, 2:-2, 2:-2] + padded[4:, 2:-2, 2:-2]
    far = far + padded[2:-2, :-4, 2:-2] + padded[2:-2, 4:, 2:-2]
    far = far + padded[2:-2, 2:-2, :-4] + padded[2:-2, 2:-2, 4:]
    return 3.0 * centre_coef * core + near_coef * near + far_coef * far


def per_device(fwd_prev, fwd_now, adj_late, adj_last, speed_model, anchors, traces, dest, rec_pos):
    prev, now = (fwd_prev[0], fwd_now[0])
    late, last = (adj_late[0], adj_last[0])
    aper_rows, slab_cols, depth = now.shape
    shot_count = lax.axis_size("shot")
    slab_count = lax.axis_size("slab")
    device_count = shot_count * slab_count
    anchor = jnp.sum(
        jnp.where(
            jnp.arange(anchors.shape[0], dtype=jnp.int32) == lax.axis_index("shot"), anchors, 0
        )
    )
    piece = lax.all_gather(speed_model, "shot", axis=0, tiled=True)
    relative = anchor + jnp.arange(aper_rows, dtype=jnp.int32)
    inside = (relative >= 0) & (relative < piece.shape[0])
    picked = jnp.take(piece, jnp.clip(relative, 0, piece.shape[0] - 1), axis=0)
    speed = jnp.where(
        inside[:, None, None], picked, jnp.zeros((aper_rows, slab_cols, depth), jnp.float32)
    )
    target = dest[:, 0]
    onehot = (target[:, None] == jnp.arange(device_count, dtype=jnp.int32)[None, :]).astype(
        jnp.int32
    )
    rank = jnp.sum(onehot * (jnp.cumsum(onehot, axis=0) - 1), axis=1)
    slot = target * CAP + rank
    sample_buf = jnp.zeros((NSTEP, device_count * CAP), jnp.float32).at[:, slot].set(traces)
    place_buf = jnp.zeros((1, device_count * CAP), jnp.int32).at[0, slot].set(rec_pos)
    got_samples, got_places = (
        lax.all_to_all(sample_buf, ("shot", "slab"), split_axis=1, concat_axis=1, tiled=True),
        lax.all_to_all(place_buf, ("shot", "slab"), split_axis=1, concat_axis=1, tiled=True),
    )
    planes = (
        jnp.zeros((NSTEP, aper_rows * slab_cols), jnp.float32).at[:, got_places[0]].add(got_samples)
    )
    planes = planes.reshape(NSTEP, aper_rows, slab_cols)

    def forward_step(carry, unused):
        older, newer = carry
        extended = extended_2(newer, (("slab", 1),), 2)
        nxt = 2.0 * newer - older + speed * laplace(extended)
        return ((newer, nxt), nxt)

    unused_carry, snaps = lax.scan(forward_step, (prev, now), None, length=NSTEP)

    def adjoint_step(carry, inputs):
        older, newer, partial_value = carry
        snap, plane = inputs
        extended = extended_2(newer, (("slab", 1),), 2)
        drive = laplace(extended).at[:, :, RDEPTH].add(plane)
        current = 2.0 * newer - older + speed * drive
        return ((newer, current, partial_value + snap * current), None)

    start_carry = (late, last, jnp.zeros((aper_rows, slab_cols, depth), jnp.float32))
    final_carry, unused_out = lax.scan(adjoint_step, start_carry, (snaps[::-1], planes[::-1]))
    partial_value = final_carry[2]
    relative = jnp.arange(speed_model.shape[0] * lax.axis_size("shot"), dtype=jnp.int32) - anchor
    inside = (relative >= 0) & (relative < aper_rows)
    picked = jnp.take(partial_value, jnp.clip(relative, 0, aper_rows - 1), axis=0)
    return lax.psum_scatter(
        jnp.where(inside[:, None, None], picked, jnp.float32(0.0)),
        "shot",
        scatter_dimension=0,
        tiled=True,
    )


def solution(mesh):
    placed = (
        P("shot", None, "slab", None),
        P("shot", None, "slab", None),
        P("shot", None, "slab", None),
        P("shot", None, "slab", None),
        P("shot", "slab", None),
        P(),
        P(None, ("shot", "slab")),
        P(("shot", "slab"), None),
        P(("shot", "slab")),
    )
    return jax.shard_map(
        per_device, mesh=mesh, in_specs=placed, out_specs=P("shot", "slab", None), check_vma=False
    )
```

profile of v0, /device:TPU:9, one launch (start us, length us, event | category | flops | bytes accessed | tf_op | source)
XLA Modules:
  0.0 929.5 jit_solution(4072706537958260280)
XLA Ops:
  59.4 379.7 %while.34 = (s32[]{:T(128)}, f32[256,16,128]{2,1,0:T(8,128)}, f32[256,16,128]{2,1,0:T(8,128)}, f32[8,256,16,128]{1,2,3,0:T(8,128)}, f32[256,16,128]{2,1,0:T(8,128)}, /*index=5*/s32[]{:T(128)}) while((s32[]{:T(128)}, f32[256,16,128]{2,1,0:T(8,128)}, f32[256,16,128]{2,1,0:T(8,128)}, f32[8,256,16,128]{1,2,3,0:T(8,128)}, ...), condition=%wide.region_2.3_spmd, body=%wide.region_1.2_spmd.sunk | while | flops 21306048 | bytes 76408280 | solution.py:87
  83.9 12.0 %fusion.52 = f32[256,16,128]{2,1,0:T(8,128)} fusion(f32[256,16,128]{2,1,0:T(8,128)} %get-tuple-element.354, f32[256,2,128]{2,1,0:T(2,128)S(1)} %collective-permute-done, f32[256,16,128]{2,1,0:T(8,128)} %get-tuple-element.346, f32[260,20,132]{2,1,0:T(8,128)S(1)} %select_maximum_fusion.6, f32[256,18,128]{2,1,0:T(8,128)} %constant_dynamic-update-slice_fusion.11, ...), kind=kLoop, calls=%fused_computation.25.clone.1 | loop fusion | flops 11010048 | bytes 29622272 | tf_op jit(solution)/shard_map/while/body/eval_jaxpr/add | solution.py:84
  118.9 6.4 collective-permute-done.1
  131.4 12.0 %fusion.52 = f32[256,16,128]{2,1,0:T(8,128)} fusion(f32[256,16,128]{2,1,0:T(8,128)} %get-tuple-element.354, f32[256,2,128]{2,1,0:T(2,128)S(1)} %collective-permute-done, f32[256,16,128]{2,1,0:T(8,128)} %get-tuple-element.346, f32[260,20,132]{2,1,0:T(8,128)S(1)} %select_maximum_fusion.6, f32[256,18,128]{2,1,0:T(8,128)} %constant_dynamic-update-slice_fusion.11, ...), kind=kLoop, calls=%fused_computation.25.clone.1 | loop fusion | flops 11010048 | bytes 29622272 | tf_op jit(solution)/shard_map/while/body/eval_jaxpr/add | solution.py:84
  178.8 12.0 %fusion.52 = f32[256,16,128]{2,1,0:T(8,128)} fusion(f32[256,16,128]{2,1,0:T(8,128)} %get-tuple-element.354, f32[256,2,128]{2,1,0:T(2,128)S(1)} %collective-permute-done, f32[256,16,128]{2,1,0:T(8,128)} %get-tuple-element.346, f32[260,20,132]{2,1,0:T(8,128)S(1)} %select_maximum_fusion.6, f32[256,18,128]{2,1,0:T(8,128)} %constant_dynamic-update-slice_fusion.11, ...), kind=kLoop, calls=%fused_computation.25.clone.1 | loop fusion | flops 11010048 | bytes 29622272 | tf_op jit(solution)/shard_map/while/body/eval_jaxpr/add | solution.py:84
  226.3 12.0 %fusion.52 = f32[256,16,128]{2,1,0:T(8,128)} fusion(f32[256,16,128]{2,1,0:T(8,128)} %get-tuple-element.354, f32[256,2,128]{2,1,0:T(2,128)S(1)} %collective-permute-done, f32[256,16,128]{2,1,0:T(8,128)} %get-tuple-element.346, f32[260,20,132]{2,1,0:T(8,128)S(1)} %select_maximum_fusion.6, f32[256,18,128]{2,1,0:T(8,128)} %constant_dynamic-update-slice_fusion.11, ...), kind=kLoop, calls=%fused_computation.25.clone.1 | loop fusion | flops 11010048 | bytes 29622272 | tf_op jit(solution)/shard_map/while/body/eval_jaxpr/add | solution.py:84
  273.8 12.0 %fusion.52 = f32[256,16,128]{2,1,0:T(8,128)} fusion(f32[256,16,128]{2,1,0:T(8,128)} %get-tuple-element.354, f32[256,2,128]{2,1,0:T(2,128)S(1)} %collective-permute-done, f32[256,16,128]{2,1,0:T(8,128)} %get-tuple-element.346, f32[260,20,132]{2,1,0:T(8,128)S(1)} %select_maximum_fusion.6, f32[256,18,128]{2,1,0:T(8,128)} %constant_dynamic-update-slice_fusion.11, ...), kind=kLoop, calls=%fused_computation.25.clone.1 | loop fusion | flops 11010048 | bytes 29622272 | tf_op jit(solution)/shard_map/while/body/eval_jaxpr/add | solution.py:84
  308.8 6.4 collective-permute-done.1
  321.3 12.0 %fusion.52 = f32[256,16,128]{2,1,0:T(8,128)} fusion(f32[256,16,128]{2,1,0:T(8,128)} %get-tuple-element.354, f32[256,2,128]{2,1,0:T(2,128)S(1)} %collective-permute-done, f32[256,16,128]{2,1,0:T(8,128)} %get-tuple-element.346, f32[260,20,132]{2,1,0:T(8,128)S(1)} %select_maximum_fusion.6, f32[256,18,128]{2,1,0:T(8,128)} %constant_dynamic-update-slice_fusion.11, ...), kind=kLoop, calls=%fused_computation.25.clone.1 | loop fusion | flops 11010048 | bytes 29622272 | tf_op jit(solution)/shard_map/while/body/eval_jaxpr/add | solution.py:84
  368.8 12.0 %fusion.52 = f32[256,16,128]{2,1,0:T(8,128)} fusion(f32[256,16,128]{2,1,0:T(8,128)} %get-tuple-element.354, f32[256,2,128]{2,1,0:T(2,128)S(1)} %collective-permute-done, f32[256,16,128]{2,1,0:T(8,128)} %get-tuple-element.346, f32[260,20,132]{2,1,0:T(8,128)S(1)} %select_maximum_fusion.6, f32[256,18,128]{2,1,0:T(8,128)} %constant_dynamic-update-slice_fusion.11, ...), kind=kLoop, calls=%fused_computation.25.clone.1 | loop fusion | flops 11010048 | bytes 29622272 | tf_op jit(solution)/shard_map/while/body/eval_jaxpr/add | solution.py:84
  416.2 12.0 %fusion.52 = f32[256,16,128]{2,1,0:T(8,128)} fusion(f32[256,16,128]{2,1,0:T(8,128)} %get-tuple-element.354, f32[256,2,128]{2,1,0:T(2,128)S(1)} %collective-permute-done, f32[256,16,128]{2,1,0:T(8,128)} %get-tuple-element.346, f32[260,20,132]{2,1,0:T(8,128)S(1)} %select_maximum_fusion.6, f32[256,18,128]{2,1,0:T(8,128)} %constant_dynamic-update-slice_fusion.11, ...), kind=kLoop, calls=%fused_computation.25.clone.1 | loop fusion | flops 11010048 | bytes 29622272 | tf_op jit(solution)/shard_map/while/body/eval_jaxpr/add | solution.py:84
  439.2 11.6 %rev.7 = f32[8,256,16,128]{1,2,3,0:T(8,128)} reverse(f32[8,256,16,128]{1,2,3,0:T(8,128)} %get-tuple-element.173), dimensions={0} | reverse | bytes 33554432 | tf_op jit(solution)/shard_map/rev | solution.py:98
  450.8 416.2 %while.35 = (s32[]{:T(128)}, f32[256,16,128]{0,1,2:T(8,128)}, f32[256,16,128]{0,1,2:T(8,128)S(1)}, f32[256,16,128]{0,1,2:T(8,128)}, f32[8,256,16]{1,2,0:T(8,128)...) while((s32[]{:T(128)}, f32[256,16,128]{0,1,2:T(8,128)}, ...), condition=%wide.region_9.10_spmd.clone, body=%wide.region_8.9_spmd.clone.sunk | while | flops 22883012 | bytes 63874500 | solution.py:98
  461.2 6.4 collective-permute-done.3
  473.1 20.0 %fusion.54 = f32[256,16,128]{0,1,2:T(8,128)} fusion(f32[256,2,128]{0,1,2:T(2,128)S(1)} %collective-permute-done.2, f32[256,16,128]{0,1,2:T(8,128)S(1)} %get-tuple-element.367, f32[260,20,132]{0,1,2:T(8,128)} %select_maximum_fusion.7, f32[256,18,128]{0,1,2:T(8,128)} %constant_dynamic-update-slice_fusion.14), kind=kLoop, calls=%fused_computation.55.clone.1 | loop fusion | flops 8912896 | bytes 25427968 | tf_op jit(solution)/shard_map/while/body/eval_jaxpr/add | solution.py:42
  494.3 6.4 fusion.56
  524.5 20.0 %fusion.54 = f32[256,16,128]{0,1,2:T(8,128)} fusion(f32[256,2,128]{0,1,2:T(2,128)S(1)} %collective-permute-done.2, f32[256,16,128]{0,1,2:T(8,128)S(1)} %get-tuple-element.367, f32[260,20,132]{0,1,2:T(8,128)} %select_maximum_fusion.7, f32[256,18,128]{0,1,2:T(8,128)} %constant_dynamic-update-slice_fusion.14), kind=kLoop, calls=%fused_computation.55.clone.1 | loop fusion | flops 8912896 | bytes 25427968 | tf_op jit(solution)/shard_map/while/body/eval_jaxpr/add | solution.py:42
  545.8 7.1 fusion.56
  576.6 20.0 %fusion.54 = f32[256,16,128]{0,1,2:T(8,128)} fusion(f32[256,2,128]{0,1,2:T(2,128)S(1)} %collective-permute-done.2, f32[256,16,128]{0,1,2:T(8,128)S(1)} %get-tuple-element.367, f32[260,20,132]{0,1,2:T(8,128)} %select_maximum_fusion.7, f32[256,18,128]{0,1,2:T(8,128)} %constant_dynamic-update-slice_fusion.14), kind=kLoop, calls=%fused_computation.55.clone.1 | loop fusion | flops 8912896 | bytes 25427968 | tf_op jit(solution)/shard_map/while/body/eval_jaxpr/add | solution.py:42
  597.9 7.0 fusion.56
  628.7 20.0 %fusion.54 = f32[256,16,128]{0,1,2:T(8,128)} fusion(f32[256,2,128]{0,1,2:T(2,128)S(1)} %collective-permute-done.2, f32[256,16,128]{0,1,2:T(8,128)S(1)} %get-tuple-element.367, f32[260,20,132]{0,1,2:T(8,128)} %select_maximum_fusion.7, f32[256,18,128]{0,1,2:T(8,128)} %constant_dynamic-update-slice_fusion.14), kind=kLoop, calls=%fused_computation.55.clone.1 | loop fusion | flops 8912896 | bytes 25427968 | tf_op jit(solution)/shard_map/while/body/eval_jaxpr/add | solution.py:42
  650.0 7.0 fusion.56
  680.8 20.0 %fusion.54 = f32[256,16,128]{0,1,2:T(8,128)} fusion(f32[256,2,128]{0,1,2:T(2,128)S(1)} %collective-permute-done.2, f32[256,16,128]{0,1,2:T(8,128)S(1)} %get-tuple-element.367, f32[260,20,132]{0,1,2:T(8,128)} %select_maximum_fusion.7, f32[256,18,128]{0,1,2:T(8,128)} %constant_dynamic-update-slice_fusion.14), kind=kLoop, calls=%fused_computation.55.clone.1 | loop fusion | flops 8912896 | bytes 25427968 | tf_op jit(solution)/shard_map/while/body/eval_jaxpr/add | solution.py:42
  702.1 7.1 fusion.56
  733.0 20.0 %fusion.54 = f32[256,16,128]{0,1,2:T(8,128)} fusion(f32[256,2,128]{0,1,2:T(2,128)S(1)} %collective-permute-done.2, f32[256,16,128]{0,1,2:T(8,128)S(1)} %get-tuple-element.367, f32[260,20,132]{0,1,2:T(8,128)} %select_maximum_fusion.7, f32[256,18,128]{0,1,2:T(8,128)} %constant_dynamic-update-slice_fusion.14), kind=kLoop, calls=%fused_computation.55.clone.1 | loop fusion | flops 8912896 | bytes 25427968 | tf_op jit(solution)/shard_map/while/body/eval_jaxpr/add | solution.py:42
  754.3 7.0 fusion.56
  785.1 20.0 %fusion.54 = f32[256,16,128]{0,1,2:T(8,128)} fusion(f32[256,2,128]{0,1,2:T(2,128)S(1)} %collective-permute-done.2, f32[256,16,128]{0,1,2:T(8,128)S(1)} %get-tuple-element.367, f32[260,20,132]{0,1,2:T(8,128)} %select_maximum_fusion.7, f32[256,18,128]{0,1,2:T(8,128)} %constant_dynamic-update-slice_fusion.14), kind=kLoop, calls=%fused_computation.55.clone.1 | loop fusion | flops 8912896 | bytes 25427968 | tf_op jit(solution)/shard_map/while/body/eval_jaxpr/add | solution.py:42
  806.3 7.0 fusion.56
  837.2 20.0 %fusion.54 = f32[256,16,128]{0,1,2:T(8,128)} fusion(f32[256,2,128]{0,1,2:T(2,128)S(1)} %collective-permute-done.2, f32[256,16,128]{0,1,2:T(8,128)S(1)} %get-tuple-element.367, f32[260,20,132]{0,1,2:T(8,128)} %select_maximum_fusion.7, f32[256,18,128]{0,1,2:T(8,128)} %constant_dynamic-update-slice_fusion.14), kind=kLoop, calls=%fused_computation.55.clone.1 | loop fusion | flops 8912896 | bytes 25427968 | tf_op jit(solution)/shard_map/while/body/eval_jaxpr/add | solution.py:42
  858.4 7.0 fusion.56
  872.6 6.6 select_select_fusion
  879.2 43.5 %reduce-scatter.2.cloned.1.call-done = f32[128,16,128]{2,1,0:T(8,128)} async-done(((f32[512,16,128]{2,1,0:T(8,128)}), f32[128,16,128]{2,1,0:T(8,128)}) %reduce-scatter.2.cloned.1.call-update) | async-done | bytes 1048592 | tf_op jit(solution)/shard_map/reduce_scatter | solution.py:103
  (269 shorter events, 523.0 us)
Async XLA Ops:
  6.5 41.2 %all-gather.2.cloned.1.call-start = ((), (), s32[]{:S(2)}) async-start(), calls=%async_computation.3 | async-start | bytes 5242880 | tf_op jit(solution)/shard_map/all_gather | solution.py:57
  13.0 17.7 %all-to-all-start = ((s32[1,32,2]{2,0,1:T(1,128)}), s32[1,32,2]{2,0,1:T(1,128)S(1)}, u32[]{:S(2)}, u32[]{:S(2)}) async-start(s32[1,32,2]{2,0,1:T(1,128)} %bitcast.6), calls=%async_computation | async-start | bytes 32768 | tf_op jit(solution)/shard_map/all_to_all | solution.py:74
  30.7 11.7 %all-to-all-start.1 = ((f32[8,32,2]{0,2,1:T(2,128)}), f32[8,32,2]{0,2,1:T(2,128)S(1)}, u32[]{:S(2)}, u32[]{:S(2)}) async-start(f32[8,32,2]{0,2,1:T(2,128)} %bitcast.9), calls=%async_computation.1 | async-start | bytes 65536 | tf_op jit(solution)/shard_map/all_to_all | solution.py:73
  36.6 886.1 %reduce-scatter.2.cloned.1.call-start = ((), (), s32[]{:S(2)}) async-start(), calls=%async_computation.4 | async-start | bytes 5242880 | tf_op jit(solution)/shard_map/reduce_scatter | solution.py:103
  61.2 14.1 %collective-permute-start = (f32[256,2,128]{2,1,0:T(2,128)S(1)}, f32[256,2,128]{2,1,0:T(2,128)S(1)}, u32[]{:S(2)}, u32[]{:S(2)}) collective-permute-start(f32[256,2,128]{2,1,0:T(2,128)S(1)} %get-tuple-element.325), channel_id=1, source_target_pairs={{0,1},{1,2},{2,3},{3,4},{4,5},{5,6},{6,7},{8,9},{9,10},{10,11},{11... | collective-permute-start | bytes 786440 | tf_op jit(solution)/shard_map/while/body/eval_jaxpr/ppermute | solution.py:24
  64.3 13.5 %collective-permute-start.1 = (f32[256,2,128]{2,1,0:T(2,128)S(1)}, f32[256,2,128]{2,1,0:T(2,128)S(1)}, u32[]{:S(2)}, u32[]{:S(2)}) collective-permute-start(f32[256,2,128]{2,1,0:T(2,128)S(1)} %get-tuple-element.326), channel_id=1, source_target_pairs={{1,0},{2,1},{3,2},{4,3},{5,4},{6,5},{7,6},{9,8},{10,9},{11,10},{12... | collective-permute-start | bytes 786440 | tf_op jit(solution)/shard_map/while/body/eval_jaxpr/ppermute | solution.py:26
  110.6 14.7 %collective-permute-start.1 = (f32[256,2,128]{2,1,0:T(2,128)S(1)}, f32[256,2,128]{2,1,0:T(2,128)S(1)}, u32[]{:S(2)}, u32[]{:S(2)}) collective-permute-start(f32[256,2,128]{2,1,0:T(2,128)S(1)} %get-tuple-element.326), channel_id=1, source_target_pairs={{1,0},{2,1},{3,2},{4,3},{5,4},{6,5},{7,6},{9,8},{10,9},{11,10},{12... | collective-permute-start | bytes 786440 | tf_op jit(solution)/shard_map/while/body/eval_jaxpr/ppermute | solution.py:26
  156.1 10.2 %collective-permute-start = (f32[256,2,128]{2,1,0:T(2,128)S(1)}, f32[256,2,128]{2,1,0:T(2,128)S(1)}, u32[]{:S(2)}, u32[]{:S(2)}) collective-permute-start(f32[256,2,128]{2,1,0:T(2,128)S(1)} %get-tuple-element.325), channel_id=1, source_target_pairs={{0,1},{1,2},{2,3},{3,4},{4,5},{5,6},{6,7},{8,9},{9,10},{10,11},{11... | collective-permute-start | bytes 786440 | tf_op jit(solution)/shard_map/while/body/eval_jaxpr/ppermute | solution.py:24
  158.0 14.7 %collective-permute-start.1 = (f32[256,2,128]{2,1,0:T(2,128)S(1)}, f32[256,2,128]{2,1,0:T(2,128)S(1)}, u32[]{:S(2)}, u32[]{:S(2)}) collective-permute-start(f32[256,2,128]{2,1,0:T(2,128)S(1)} %get-tuple-element.326), channel_id=1, source_target_pairs={{1,0},{2,1},{3,2},{4,3},{5,4},{6,5},{7,6},{9,8},{10,9},{11,10},{12... | collective-permute-start | bytes 786440 | tf_op jit(solution)/shard_map/while/body/eval_jaxpr/ppermute | solution.py:26
  203.5 10.2 %collective-permute-start = (f32[256,2,128]{2,1,0:T(2,128)S(1)}, f32[256,2,128]{2,1,0:T(2,128)S(1)}, u32[]{:S(2)}, u32[]{:S(2)}) collective-permute-start(f32[256,2,128]{2,1,0:T(2,128)S(1)} %get-tuple-element.325), channel_id=1, source_target_pairs={{0,1},{1,2},{2,3},{3,4},{4,5},{5,6},{6,7},{8,9},{9,10},{10,11},{11... | collective-permute-start | bytes 786440 | tf_op jit(solution)/shard_map/while/body/eval_jaxpr/ppermute | solution.py:24
  205.5 14.7 %collective-permute-start.1 = (f32[256,2,128]{2,1,0:T(2,128)S(1)}, f32[256,2,128]{2,1,0:T(2,128)S(1)}, u32[]{:S(2)}, u32[]{:S(2)}) collective-permute-start(f32[256,2,128]{2,1,0:T(2,128)S(1)} %get-tuple-element.326), channel_id=1, source_target_pairs={{1,0},{2,1},{3,2},{4,3},{5,4},{6,5},{7,6},{9,8},{10,9},{11,10},{12... | collective-permute-start | bytes 786440 | tf_op jit(solution)/shard_map/while/body/eval_jaxpr/ppermute | solution.py:26
  251.0 10.2 %collective-permute-start = (f32[256,2,128]{2,1,0:T(2,128)S(1)}, f32[256,2,128]{2,1,0:T(2,128)S(1)}, u32[]{:S(2)}, u32[]{:S(2)}) collective-permute-start(f32[256,2,128]{2,1,0:T(2,128)S(1)} %get-tuple-element.325), channel_id=1, source_target_pairs={{0,1},{1,2},{2,3},{3,4},{4,5},{5,6},{6,7},{8,9},{9,10},{10,11},{11... | collective-permute-start | bytes 786440 | tf_op jit(solution)/shard_map/while/body/eval_jaxpr/ppermute | solution.py:24
  253.0 14.7 %collective-permute-start.1 = (f32[256,2,128]{2,1,0:T(2,128)S(1)}, f32[256,2,128]{2,1,0:T(2,128)S(1)}, u32[]{:S(2)}, u32[]{:S(2)}) collective-permute-start(f32[256,2,128]{2,1,0:T(2,128)S(1)} %get-tuple-element.326), channel_id=1, source_target_pairs={{1,0},{2,1},{3,2},{4,3},{5,4},{6,5},{7,6},{9,8},{10,9},{11,10},{12... | collective-permute-start | bytes 786440 | tf_op jit(solution)/shard_map/while/body/eval_jaxpr/ppermute | solution.py:26
  298.5 10.2 %collective-permute-start = (f32[256,2,128]{2,1,0:T(2,128)S(1)}, f32[256,2,128]{2,1,0:T(2,128)S(1)}, u32[]{:S(2)}, u32[]{:S(2)}) collective-permute-start(f32[256,2,128]{2,1,0:T(2,128)S(1)} %get-tuple-element.325), channel_id=1, source_target_pairs={{0,1},{1,2},{2,3},{3,4},{4,5},{5,6},{6,7},{8,9},{9,10},{10,11},{11... | collective-permute-start | bytes 786440 | tf_op jit(solution)/shard_map/while/body/eval_jaxpr/ppermute | solution.py:24
  300.5 14.7 %collective-permute-start.1 = (f32[256,2,128]{2,1,0:T(2,128)S(1)}, f32[256,2,128]{2,1,0:T(2,128)S(1)}, u32[]{:S(2)}, u32[]{:S(2)}) collective-permute-start(f32[256,2,128]{2,1,0:T(2,128)S(1)} %get-tuple-element.326), channel_id=1, source_target_pairs={{1,0},{2,1},{3,2},{4,3},{5,4},{6,5},{7,6},{9,8},{10,9},{11,10},{12... | collective-permute-start | bytes 786440 | tf_op jit(solution)/shard_map/while/body/eval_jaxpr/ppermute | solution.py:26
  346.0 10.2 %collective-permute-start = (f32[256,2,128]{2,1,0:T(2,128)S(1)}, f32[256,2,128]{2,1,0:T(2,128)S(1)}, u32[]{:S(2)}, u32[]{:S(2)}) collective-permute-start(f32[256,2,128]{2,1,0:T(2,128)S(1)} %get-tuple-element.325), channel_id=1, source_target_pairs={{0,1},{1,2},{2,3},{3,4},{4,5},{5,6},{6,7},{8,9},{9,10},{10,11},{11... | collective-permute-start | bytes 786440 | tf_op jit(solution)/shard_map/while/body/eval_jaxpr/ppermute | solution.py:24
  347.9 14.7 %collective-permute-start.1 = (f32[256,2,128]{2,1,0:T(2,128)S(1)}, f32[256,2,128]{2,1,0:T(2,128)S(1)}, u32[]{:S(2)}, u32[]{:S(2)}) collective-permute-start(f32[256,2,128]{2,1,0:T(2,128)S(1)} %get-tuple-element.326), channel_id=1, source_target_pairs={{1,0},{2,1},{3,2},{4,3},{5,4},{6,5},{7,6},{9,8},{10,9},{11,10},{12... | collective-permute-start | bytes 786440 | tf_op jit(solution)/shard_map/while/body/eval_jaxpr/ppermute | solution.py:26
  393.5 10.2 %collective-permute-start = (f32[256,2,128]{2,1,0:T(2,128)S(1)}, f32[256,2,128]{2,1,0:T(2,128)S(1)}, u32[]{:S(2)}, u32[]{:S(2)}) collective-permute-start(f32[256,2,128]{2,1,0:T(2,128)S(1)} %get-tuple-element.325), channel_id=1, source_target_pairs={{0,1},{1,2},{2,3},{3,4},{4,5},{5,6},{6,7},{8,9},{9,10},{10,11},{11... | collective-permute-start | bytes 786440 | tf_op jit(solution)/shard_map/while/body/eval_jaxpr/ppermute | solution.py:24
  395.4 14.7 %collective-permute-start.1 = (f32[256,2,128]{2,1,0:T(2,128)S(1)}, f32[256,2,128]{2,1,0:T(2,128)S(1)}, u32[]{:S(2)}, u32[]{:S(2)}) collective-permute-start(f32[256,2,128]{2,1,0:T(2,128)S(1)} %get-tuple-element.326), channel_id=1, source_target_pairs={{1,0},{2,1},{3,2},{4,3},{5,4},{6,5},{7,6},{9,8},{10,9},{11,10},{12... | collective-permute-start | bytes 786440 | tf_op jit(solution)/shard_map/while/body/eval_jaxpr/ppermute | solution.py:26
  450.9 10.2 %collective-permute-start.2 = (f32[256,2,128]{0,1,2:T(2,128)S(1)}, f32[256,2,128]{0,1,2:T(2,128)S(1)}, u32[]{:S(2)}, u32[]{:S(2)}) collective-permute-start(f32[256,2,128]{0,1,2:T(2,128)S(1)} %get-tuple-element.334), channel_id=1, source_target_pairs={{0,1},{1,2},{2,3},{3,4},{4,5},{5,6},{6,7},{8,9},{9,10},{10,11},{11... | collective-permute-start | bytes 786440 | tf_op jit(solution)/shard_map/while/body/eval_jaxpr/ppermute | solution.py:24
  452.9 14.7 %collective-permute-start.3 = (f32[256,2,128]{0,1,2:T(2,128)S(1)}, f32[256,2,128]{0,1,2:T(2,128)S(1)}, u32[]{:S(2)}, u32[]{:S(2)}) collective-permute-start(f32[256,2,128]{0,1,2:T(2,128)S(1)} %get-tuple-element.335), channel_id=1, source_target_pairs={{1,0},{2,1},{3,2},{4,3},{5,4},{6,5},{7,6},{9,8},{10,9},{11,10},{12... | collective-permute-start | bytes 786440 | tf_op jit(solution)/shard_map/while/body/eval_jaxpr/ppermute | solution.py:26
  504.4 14.7 %collective-permute-start.3 = (f32[256,2,128]{0,1,2:T(2,128)S(1)}, f32[256,2,128]{0,1,2:T(2,128)S(1)}, u32[]{:S(2)}, u32[]{:S(2)}) collective-permute-start(f32[256,2,128]{0,1,2:T(2,128)S(1)} %get-tuple-element.335), channel_id=1, source_target_pairs={{1,0},{2,1},{3,2},{4,3},{5,4},{6,5},{7,6},{9,8},{10,9},{11,10},{12... | collective-permute-start | bytes 786440 | tf_op jit(solution)/shard_map/while/body/eval_jaxpr/ppermute | solution.py:26
  554.5 10.2 %collective-permute-start.2 = (f32[256,2,128]{0,1,2:T(2,128)S(1)}, f32[256,2,128]{0,1,2:T(2,128)S(1)}, u32[]{:S(2)}, u32[]{:S(2)}) collective-permute-start(f32[256,2,128]{0,1,2:T(2,128)S(1)} %get-tuple-element.334), channel_id=1, source_target_pairs={{0,1},{1,2},{2,3},{3,4},{4,5},{5,6},{6,7},{8,9},{9,10},{10,11},{11... | collective-permute-start | bytes 786440 | tf_op jit(solution)/shard_map/while/body/eval_jaxpr/ppermute | solution.py:24
  556.5 14.7 %collective-permute-start.3 = (f32[256,2,128]{0,1,2:T(2,128)S(1)}, f32[256,2,128]{0,1,2:T(2,128)S(1)}, u32[]{:S(2)}, u32[]{:S(2)}) collective-permute-start(f32[256,2,128]{0,1,2:T(2,128)S(1)} %get-tuple-element.335), channel_id=1, source_target_pairs={{1,0},{2,1},{3,2},{4,3},{5,4},{6,5},{7,6},{9,8},{10,9},{11,10},{12... | collective-permute-start | bytes 786440 | tf_op jit(solution)/shard_map/while/body/eval_jaxpr/ppermute | solution.py:26
  608.6 14.7 %collective-permute-start.3 = (f32[256,2,128]{0,1,2:T(2,128)S(1)}, f32[256,2,128]{0,1,2:T(2,128)S(1)}, u32[]{:S(2)}, u32[]{:S(2)}) collective-permute-start(f32[256,2,128]{0,1,2:T(2,128)S(1)} %get-tuple-element.335), channel_id=1, source_target_pairs={{1,0},{2,1},{3,2},{4,3},{5,4},{6,5},{7,6},{9,8},{10,9},{11,10},{12... | collective-permute-start | bytes 786440 | tf_op jit(solution)/shard_map/while/body/eval_jaxpr/ppermute | solution.py:26
  658.7 10.2 %collective-permute-start.2 = (f32[256,2,128]{0,1,2:T(2,128)S(1)}, f32[256,2,128]{0,1,2:T(2,128)S(1)}, u32[]{:S(2)}, u32[]{:S(2)}) collective-permute-start(f32[256,2,128]{0,1,2:T(2,128)S(1)} %get-tuple-element.334), channel_id=1, source_target_pairs={{0,1},{1,2},{2,3},{3,4},{4,5},{5,6},{6,7},{8,9},{9,10},{10,11},{11... | collective-permute-start | bytes 786440 | tf_op jit(solution)/shard_map/while/body/eval_jaxpr/ppermute | solution.py:24
  660.6 14.7 %collective-permute-start.3 = (f32[256,2,128]{0,1,2:T(2,128)S(1)}, f32[256,2,128]{0,1,2:T(2,128)S(1)}, u32[]{:S(2)}, u32[]{:S(2)}) collective-permute-start(f32[256,2,128]{0,1,2:T(2,128)S(1)} %get-tuple-element.335), channel_id=1, source_target_pairs={{1,0},{2,1},{3,2},{4,3},{5,4},{6,5},{7,6},{9,8},{10,9},{11,10},{12... | collective-permute-start | bytes 786440 | tf_op jit(solution)/shard_map/while/body/eval_jaxpr/ppermute | solution.py:26
  710.9 10.2 %collective-permute-start.2 = (f32[256,2,128]{0,1,2:T(2,128)S(1)}, f32[256,2,128]{0,1,2:T(2,128)S(1)}, u32[]{:S(2)}, u32[]{:S(2)}) collective-permute-start(f32[256,2,128]{0,1,2:T(2,128)S(1)} %get-tuple-element.334), channel_id=1, source_target_pairs={{0,1},{1,2},{2,3},{3,4},{4,5},{5,6},{6,7},{8,9},{9,10},{10,11},{11... | collective-permute-start | bytes 786440 | tf_op jit(solution)/shard_map/while/body/eval_jaxpr/ppermute | solution.py:24
  712.8 14.7 %collective-permute-start.3 = (f32[256,2,128]{0,1,2:T(2,128)S(1)}, f32[256,2,128]{0,1,2:T(2,128)S(1)}, u32[]{:S(2)}, u32[]{:S(2)}) collective-permute-start(f32[256,2,128]{0,1,2:T(2,128)S(1)} %get-tuple-element.335), channel_id=1, source_target_pairs={{1,0},{2,1},{3,2},{4,3},{5,4},{6,5},{7,6},{9,8},{10,9},{11,10},{12... | collective-permute-start | bytes 786440 | tf_op jit(solution)/shard_map/while/body/eval_jaxpr/ppermute | solution.py:26
  763.0 10.2 %collective-permute-start.2 = (f32[256,2,128]{0,1,2:T(2,128)S(1)}, f32[256,2,128]{0,1,2:T(2,128)S(1)}, u32[]{:S(2)}, u32[]{:S(2)}) collective-permute-start(f32[256,2,128]{0,1,2:T(2,128)S(1)} %get-tuple-element.334), channel_id=1, source_target_pairs={{0,1},{1,2},{2,3},{3,4},{4,5},{5,6},{6,7},{8,9},{9,10},{10,11},{11... | collective-permute-start | bytes 786440 | tf_op jit(solution)/shard_map/while/body/eval_jaxpr/ppermute | solution.py:24
  764.9 14.7 %collective-permute-start.3 = (f32[256,2,128]{0,1,2:T(2,128)S(1)}, f32[256,2,128]{0,1,2:T(2,128)S(1)}, u32[]{:S(2)}, u32[]{:S(2)}) collective-permute-start(f32[256,2,128]{0,1,2:T(2,128)S(1)} %get-tuple-element.335), channel_id=1, source_target_pairs={{1,0},{2,1},{3,2},{4,3},{5,4},{6,5},{7,6},{9,8},{10,9},{11,10},{12... | collective-permute-start | bytes 786440 | tf_op jit(solution)/shard_map/while/body/eval_jaxpr/ppermute | solution.py:26
  817.0 14.7 %collective-permute-start.3 = (f32[256,2,128]{0,1,2:T(2,128)S(1)}, f32[256,2,128]{0,1,2:T(2,128)S(1)}, u32[]{:S(2)}, u32[]{:S(2)}) collective-permute-start(f32[256,2,128]{0,1,2:T(2,128)S(1)} %get-tuple-element.335), channel_id=1, source_target_pairs={{1,0},{2,1},{3,2},{4,3},{5,4},{6,5},{7,6},{9,8},{10,9},{11,10},{12... | collective-permute-start | bytes 786440 | tf_op jit(solution)/shard_map/while/body/eval_jaxpr/ppermute | solution.py:26
  (27 other events, 187.4 us)
Sparse Core Ops, SparseCore 0:
  11.3 36.4 all-gather.1
  879.3 43.3 reduce-scatter.1
where the time goes:
time: 934 us; the launch traced here: 930 us
  other arithmetic  420 us (45%)
  local copies, waits for them, and re-layouts  207 us (22%)
  waiting for transfers between devices  177 us (19%)
  starting transfers between devices  111 us (12%)
  between operations  13.6 us (1%)
    add x8, other arithmetic, laplace(): return 3.0 * centre_coef * core + near_coef * near + far_coef * far  160 us
    while x80, local copies, waits for them, and re-layouts  100 us
    ppermute x16, waiting for transfers between devices, extended_2(): lax.ppermute(head, axis, [((i + 1) % count, i) for i in range(ends)])  98.8 us
    add x8, other arithmetic, forward_step(): nxt = 2.0 * newer - older + speed * laplace(extended)  95.9 us
    concatenate x16, other arithmetic, extended_2(): jnp.concatenate([lax.ppermute(tail, axis, [(i, (i + 1) % count) for i in...  79.5 us
    ppermute x16, starting transfers between devices, extended_2(): lax.ppermute(head, axis, [((i + 1) % count, i) for i in range(ends)])  67 us
    add x8, other arithmetic, adjoint_step(): return ((newer, current, partial_value + snap * current), None)  55.8 us
    reduce_scatter x1, waiting for transfers between devices, per_device(): lax.psum_scatter(jnp.where(inside[:, None, None], picked, jnp.float32(0.0...  43.5 us
  transfers between devices with their start and end apart: 36, of which 35 were waited for; matrix products, arithmetic and copies ran while one was open for 6% of the time, Pallas kernels for 0%

commit v1 on v0

v1 whole, which is shorter than its diff:
```python
import functools

import jax
import jax.numpy as jnp
from jax import lax
from jax.experimental import pallas as pl
from jax.experimental.pallas import tpu as pltpu
from jax.sharding import PartitionSpec as P

NSTEP = 8
HALF = NSTEP // 2
CAP = 2
RDEPTH = 3
ROWS = 4
CHUNKS = 2
SLOTS = HALF + 2

centre_coef = -2.5
near_coef = 4.0 / 3.0
far_coef = -1.0 / 12.0

MESH = pl.DeviceIdType.MESH


def slot_of(n):
    late = (n + 1) // SLOTS
    return (n + 1) * (1 - late) + ((n + 1) % 2) * late


def wave_kernel(
    fwd_prev, fwd_now, adj_late, adj_last, speed_in, drive_in,
    out_ref,
    field, halo, edge, speed, drive,
    load_sem, send_sem, recv_sem,
):
    count = lax.axis_size("slab")
    me = lax.axis_index("slab")
    shot = lax.axis_index("shot")
    rows, cells, depth = speed.shape
    part = rows // CHUNKS

    loads = [
        pltpu.make_async_copy(fwd_now, field.at[0, 1, pl.ds(2, rows)], load_sem.at[0]),
        pltpu.make_async_copy(adj_last, field.at[1, 1, pl.ds(2, rows)], load_sem.at[1]),
        pltpu.make_async_copy(fwd_prev, field.at[0, 0, pl.ds(2, rows)], load_sem.at[2]),
        pltpu.make_async_copy(speed_in, speed, load_sem.at[3]),
        pltpu.make_async_copy(adj_late, field.at[1, 0, pl.ds(2, rows)], load_sem.at[4]),
        pltpu.make_async_copy(drive_in, drive, load_sem.at[5]),
    ]
    for load in loads:
        load.start()

    barrier = pltpu.get_barrier_semaphore()

    @pl.when(me > 0)
    def _():
        pl.semaphore_signal(barrier, inc=1, device_id=(shot, me - 1), device_id_type=MESH)

    @pl.when(me < count - 1)
    def _():
        pl.semaphore_signal(barrier, inc=1, device_id=(shot, me + 1), device_id_type=MESH)

    border = jnp.zeros((2, cells, depth), jnp.float32)
    for which in range(2):
        for slot in range(SLOTS):
            field[which, slot, 0:2] = border
            field[which, slot, rows + 2 : rows + 4] = border

    def clear(side):
        def body(i, carry):
            for which in range(2):
                for step in range(NSTEP):
                    halo[which, step, side, pl.ds(i * 16, 16)] = jnp.zeros(
                        (16, 2, depth), jnp.float32
                    )
            return carry

        lax.fori_loop(0, rows // 16, body, 0)

    @pl.when(me == 0)
    def _():
        clear(0)

    @pl.when(me == count - 1)
    def _():
        clear(1)

    peers = (me + count - 1) // count + (2 * count - 2 - me) // count
    pl.semaphore_wait(barrier, peers)

    def transfer(which, step, side, chunk):
        span = pl.ds(chunk * part, part)
        return pltpu.make_async_remote_copy(
            src_ref=edge.at[which, step, side, span],
            dst_ref=halo.at[which, step, 1 - side, span],
            send_sem=send_sem.at[which, step, side, chunk],
            recv_sem=recv_sem.at[which, step, 1 - side, chunk],
            device_id=(shot, me - 1 + 2 * side),
            device_id_type=MESH,
        )

    def send(which, step, chunk):
        @pl.when(me > 0)
        def _():
            transfer(which, step, 0, chunk).start()

        @pl.when(me < count - 1)
        def _():
            transfer(which, step, 1, chunk).start()

    def receive(which, step, chunk):
        @pl.when(me > 0)
        def _():
            transfer(which, step, 1, chunk).wait_recv()

        @pl.when(me < count - 1)
        def _():
            transfer(which, step, 0, chunk).wait_recv()

    for which in range(2):
        loads[which].wait()
        for chunk in range(CHUNKS):
            def pack(i, carry):
                y = chunk * part + i * 8
                cell = field[which, 1, pl.ds(y + 2, 8)]
                edge[which, 0, 0, pl.ds(y, 8)] = cell[:, 0:2]
                edge[which, 0, 1, pl.ds(y, 8)] = cell[:, cells - 2 : cells]
                return carry

            lax.fori_loop(0, part // 8, pack, 0)
            send(which, 0, chunk)

    for load in loads[2:]:
        load.wait()

    lane = lax.broadcasted_iota(jnp.int32, (ROWS, cells, depth), 2)

    def advance(which, k, image, last):
        newer, older, target = slot_of(k - 1), slot_of(k - 2), slot_of(k)
        partner = slot_of(k) if which == 0 else slot_of(NSTEP + 1 - k)
        for chunk in range(CHUNKS):
            receive(which, k - 1, chunk)

            def body(i, carry):
                y = chunk * part + i * ROWS
                window = field[which, newer, pl.ds(y, ROWS + 4)]
                core = window[2 : ROWS + 2]
                left = halo[which, k - 1, 0, pl.ds(y, ROWS)]
                right = halo[which, k - 1, 1, pl.ds(y, ROWS)]
                near = window[1 : ROWS + 1] + window[3 : ROWS + 3]
                far = window[0:ROWS] + window[4 : ROWS + 4]
                near = near + jnp.concatenate([left[:, 1:2], core[:, : cells - 1]], axis=1)
                near = near + jnp.concatenate([core[:, 1:], right[:, 0:1]], axis=1)
                far = far + jnp.concatenate([left, core[:, : cells - 2]], axis=1)
                far = far + jnp.concatenate([core[:, 2:], right], axis=1)
                near = near + jnp.where(lane >= 1, pltpu.roll(core, 1, 2), 0.0)
                near = near + jnp.where(lane < depth - 1, pltpu.roll(core, depth - 1, 2), 0.0)
                far = far + jnp.where(lane >= 2, pltpu.roll(core, 2, 2), 0.0)
                far = far + jnp.where(lane < depth - 2, pltpu.roll(core, depth - 2, 2), 0.0)
                lap = 3.0 * centre_coef * core + near_coef * near + far_coef * far
                if which == 1:
                    samples = drive[pl.ds(y, ROWS)]
                    shift = (RDEPTH - NSTEP + k + depth) % depth
                    lap = lap + jnp.where(lane == RDEPTH, pltpu.roll(samples, shift, 2), 0.0)
                older_cell = field[which, older, pl.ds(y + 2, ROWS)]
                value = 2.0 * core - older_cell + speed[pl.ds(y, ROWS)] * lap
                if image:
                    if which == 0:
                        other = field[1, slot_of(NSTEP + 1 - k), pl.ds(y + 2, ROWS)]
                    else:
                        other = field[0, slot_of(NSTEP + 1 - k), pl.ds(y + 2, ROWS)]
                    if image == "first" and which == 0:
                        out_ref[pl.ds(y, ROWS)] = value * other
                    else:
                        out_ref[pl.ds(y, ROWS)] = out_ref[pl.ds(y, ROWS)] + value * other
                if not last:
                    field[which, target, pl.ds(y + 2, ROWS)] = value
                    edge[which, k, 0, pl.ds(y, ROWS)] = value[:, 0:2]
                    edge[which, k, 1, pl.ds(y, ROWS)] = value[:, cells - 2 : cells]
                return carry

            lax.fori_loop(0, part // ROWS, body, 0)
            if not last:
                send(which, k, chunk)

    def early(k, carry):
        advance(0, k, None, False)
        advance(1, k, None, False)
        return carry

    lax.fori_loop(1, HALF + 1, early, 0)
    advance(0, HALF + 1, "first", False)
    advance(1, HALF + 1, "first", False)

    def later(k, carry):
        advance(0, k, "more", False)
        advance(1, k, "more", False)
        return carry

    lax.fori_loop(HALF + 2, NSTEP, later, 0)
    advance(0, NSTEP, "more", True)
    advance(1, NSTEP, "more", True)

    def settle(step, carry):
        for which in range(2):
            for chunk in range(CHUNKS):
                @pl.when(me > 0)
                def _():
                    transfer(which, step, 0, chunk).wait_send()

                @pl.when(me < count - 1)
                def _():
                    transfer(which, step, 1, chunk).wait_send()

        return carry

    lax.fori_loop(0, NSTEP, settle, 0)


def waves(prev, now, late, last, speed, drive):
    rows, cells, depth = now.shape
    anywhere = pl.BlockSpec(memory_space=pl.ANY)
    return pl.pallas_call(
        wave_kernel,
        out_shape=jax.ShapeDtypeStruct((rows, cells, depth), jnp.float32),
        in_specs=[anywhere] * 6,
        out_specs=pl.BlockSpec(memory_space=pltpu.VMEM),
        scratch_shapes=[
            pltpu.VMEM((2, SLOTS, rows + 4, cells, depth), jnp.float32),
            pltpu.VMEM((2, NSTEP, 2, rows, 2, depth), jnp.float32),
            pltpu.VMEM((2, NSTEP, 2, rows, 2, depth), jnp.float32),
            pltpu.VMEM((rows, cells, depth), jnp.float32),
            pltpu.VMEM((rows, cells, depth), jnp.float32),
            pltpu.SemaphoreType.DMA((6,)),
            pltpu.SemaphoreType.DMA((2, NSTEP, 2, CHUNKS)),
            pltpu.SemaphoreType.DMA((2, NSTEP, 2, CHUNKS)),
        ],
        compiler_params=pltpu.CompilerParams(
            collective_id=0, has_side_effects=True, vmem_limit_bytes=60 * 1024 * 1024
        ),
        name="waves",
    )(prev, now, late, last, speed, drive)


def per_device(fwd_prev, fwd_now, adj_late, adj_last, speed_model, anchors, traces, dest, rec_pos):
    prev, now = (fwd_prev[0], fwd_now[0])
    late, last = (adj_late[0], adj_last[0])
    aper_rows, slab_cols, depth = now.shape
    device_count = lax.axis_size("shot") * lax.axis_size("slab")
    anchor = lax.dynamic_index_in_dim(anchors, lax.axis_index("shot"), keepdims=False)
    piece = lax.all_gather(speed_model, "shot", axis=0, tiled=True)
    speed = lax.dynamic_slice_in_dim(piece, anchor, aper_rows, axis=0)

    target = dest[:, 0]
    onehot = (target[:, None] == jnp.arange(device_count, dtype=jnp.int32)[None, :]).astype(
        jnp.int32
    )
    rank = jnp.sum(onehot * (jnp.cumsum(onehot, axis=0) - 1), axis=1)
    slot = target * CAP + rank
    sample_buf = jnp.zeros((NSTEP, device_count * CAP), jnp.float32).at[:, slot].set(traces)
    place_buf = jnp.zeros((1, device_count * CAP), jnp.int32).at[0, slot].set(rec_pos)
    got_samples, got_places = (
        lax.all_to_all(sample_buf, ("shot", "slab"), split_axis=1, concat_axis=1, tiled=True),
        lax.all_to_all(place_buf, ("shot", "slab"), split_axis=1, concat_axis=1, tiled=True),
    )
    wide = jnp.pad(got_samples.T, ((0, 0), (0, depth - NSTEP)))
    drive = jnp.zeros((aper_rows * slab_cols, depth), jnp.float32).at[got_places[0]].add(wide)
    drive = drive.reshape(aper_rows, slab_cols, depth)

    partial_value = waves(prev, now, late, last, speed, drive)

    model_rows = speed_model.shape[0] * lax.axis_size("shot")
    placed = lax.dynamic_update_slice_in_dim(
        jnp.zeros((model_rows, slab_cols, depth), jnp.float32), partial_value, anchor, axis=0
    )
    return lax.psum_scatter(placed, "shot", scatter_dimension=0, tiled=True)


def solution(mesh):
    placed = (
        P("shot", None, "slab", None),
        P("shot", None, "slab", None),
        P("shot", None, "slab", None),
        P("shot", None, "slab", None),
        P("shot", "slab", None),
        P(),
        P(None, ("shot", "slab")),
        P(("shot", "slab"), None),
        P(("shot", "slab")),
    )
    return jax.shard_map(
        per_device, mesh=mesh, in_specs=placed, out_specs=P("shot", "slab", None), check_vma=False
    )
```

time: 934 us -> 302 us (0.32)
  other arithmetic: 420 us -> 5.24 us
  local copies, waits for them, and re-layouts: 207 us -> 12.3 us
  Pallas kernels: 0 us -> 193 us
  waiting for transfers between devices: 177 us -> 61.7 us
  starting transfers between devices: 111 us -> 11.9 us
    add x24 -> x0, other arithmetic: 311 us -> none  [the longest x8 160 us: laplace(): return 3.0 * centre_coef * core + near_coef * near + far_coef * far]
    pallas_call x0 -> x1, Pallas kernels: none -> 193 us  [waves(): pl.pallas_call(wave_kernel, out_shape=jax.ShapeDtypeStruct((rows, cells,...]
    ppermute x32 -> x0, waiting for transfers between devices: 129 us -> none  [the longest x16 98.8 us: extended_2(): lax.ppermute(head, axis, [((i + 1) % count, i) for i in range(ends)])]
    while x81 -> x0, local copies, waits for them, and re-layouts: 103 us -> none
    ppermute x32 -> x0, starting transfers between devices: 98.9 us -> none  [the longest x16 67 us: extended_2(): lax.ppermute(head, axis, [((i + 1) % count, i) for i in range(ends)])]
    concatenate x16 -> x0, other arithmetic: 79.5 us -> none  [extended_2(): jnp.concatenate([lax.ppermute(tail, axis, [(i, (i + 1) % count) for i in...]
    dynamic_update_slice x16 -> x1, local copies, waits for them, and re-layouts: 37.7 us -> 1.46 us  [per_device(): lax.dynamic_update_slice_in_dim(jnp.zeros((model_rows, slab_cols, depth),...]
    slice x16 -> x0, local copies, waits for them, and re-layouts: 15.2 us -> none  [extended_2(): head = lax.slice_in_dim(cells, 0, width, axis=dim)]
  transfers between devices with their start and end apart: 36 -> 4, of which waited for: 35 -> 4; matrix products, arithmetic and copies ran while one was open for 6% -> 3% of each run, Pallas kernels for 0% -> 0%
where the time goes in v1:
time: 302 us; the launch traced here: 300 us
  Pallas kernels  193 us (64%)
  waiting for transfers between devices  61.7 us (20%)
  between operations  15.4 us (5%)
  local copies, waits for them, and re-layouts  12.3 us (4%)
  starting transfers between devices  11.9 us (4%)
  other arithmetic  5.24 us (2%)
    pallas_call x1, Pallas kernels, waves(): pl.pallas_call(wave_kernel, out_shape=jax.ShapeDtypeStruct((rows, cells,...  193 us
    reduce_scatter x1, waiting for transfers between devices, per_device(): return lax.psum_scatter(placed, 'shot', scatter_dimension=0, tiled=True)  47.3 us
    all_gather x1, waiting for transfers between devices, per_device(): piece = lax.all_gather(speed_model, 'shot', axis=0, tiled=True)  8.78 us
    all_to_all x1, starting transfers between devices, per_device(): lax.all_to_all(place_buf, ('shot', 'slab'), split_axis=1, concat_axis=1,...  6.36 us
  transfers between devices with their start and end apart: 4, of which 4 were waited for; matrix products, arithmetic and copies ran while one was open for 3% of the time, Pallas kernels for 0%

profile of v1, /device:TPU:9, one launch (start us, length us, event | category | flops | bytes accessed | tf_op | source)
XLA Modules:
  0.0 299.9 jit_solution(1683636542642790318)
XLA Ops:
  6.5 0.0 all-gather.2.cloned.1.call-start
  6.5 0.7 all-gather.2.cloned.1.call-update
  7.3 0.7 fusion.5
  8.0 0.1 reduce_window_sum.11
  8.0 0.8 select_reduce_fusion
  8.9 0.7 fusion.6
  9.5 0.8 scatter_custom_fusion
  10.4 0.7 all_to_all.14
  11.1 6.4 %all-to-all-start = ((s32[1,32,2]{2,0,1:T(1,128)}), s32[1,32,2]{2,0,1:T(1,128)S(1)}, u32[]{:S(2)}, u32[]{:S(2)}) async-start(s32[1,32,2]{2,0,1:T(1,128)} %bitcast.8), calls=%async_computation | async-start | bytes 32768 | tf_op jit(solution)/shard_map/all_to_all | solution.py:264
  17.4 1.2 dynamic_slice.7
  20.0 0.8 copy.13
  21.4 1.2 scatter_custom_fusion.1
  22.7 0.3 all-to-all-done
  23.0 5.5 %all-to-all-start.1 = ((f32[8,32,2]{0,2,1:T(2,128)}), f32[8,32,2]{0,2,1:T(2,128)S(1)}, u32[]{:S(2)}, u32[]{:S(2)}) async-start(f32[8,32,2]{0,2,1:T(2,128)} %bitcast.11), calls=%async_computation.1 | async-start | bytes 65536 | tf_op jit(solution)/shard_map/all_to_all | solution.py:263
  28.5 0.0 reduce-scatter.2.cloned.1.call-start
  28.5 0.5 broadcast.54
  29.1 0.7 reduce.3
  29.7 0.1 squeeze.25
  29.8 4.5 %all-to-all-done.1 = f32[8,32,2]{0,2,1:T(2,128)S(1)} async-done(((f32[8,32,2]{0,2,1:T(2,128)}), f32[8,32,2]{0,2,1:T(2,128)S(1)}, u32[]{:S(2)}, u32[]{:S(2)}) %all-to-all-start.1) | async-done | bytes 2080 | tf_op jit(solution)/shard_map/all_to_all | solution.py:263
  34.4 2.3 scatter_custom_fusion.2
  36.7 8.8 %all-gather.2.cloned.1.call-done = f32[512,16,128]{2,1,0:T(8,128)} async-done(((f32[128,16,128]{2,1,0:T(8,128)}), f32[512,16,128]{2,1,0:T(8,128)}) %all-gather.2.cloned.1.call-update) | async-done | bytes 4194320 | tf_op jit(solution)/shard_map/all_gather | solution.py:251
  45.4 3.1 %constant_dynamic-slice_fusion.speed_in = f32[256,16,128]{2,1,0:T(8,128)} fusion(f32[512,16,128]{2,1,0:T(8,128)} %all-gather.2.cloned.1.call-done, s32[]{:T(128)S(6)} %select_n.24), kind=kLoop, calls=%fused_computation.17 | loop fusion | bytes 4194308 | tf_op jit(solution)/shard_map/dynamic_slice | solution.py:252
  48.5 193.3 %waves.1 = f32[256,16,128]{2,1,0:T(8,128)} custom-call(f32[256,16,128]{2,1,0:T(8,128)} %bitcast.25, f32[256,16,128]{2,1,0:T(8,128)} %bitcast.26, f32[256,16,128]{2,1,0:T(8,128)} %bitcast.27, f32[256,16,128]{2,1,0:T(8,128)} %bitcast.28, f32[256,16,128]{2,1,0:T(8,128)} %constant_dynamic-slice_fusion.speed_in, f32[256,16,128]{2,1,0:T(8,128)} %bitcast.24), custom_call_target="tpu_custom_call" | custom-call | tf_op jit(solution)/shard_map/waves/pallas_call | solution.py:223
  241.8 0.0 copy-start
  241.8 2.2 broadcast_in_dim.8
  244.0 0.2 copy-done
  244.2 1.5 constant_dynamic-update-slice_fusion
  245.7 0.0 reduce-scatter.2.cloned.1.call-update
  245.7 47.3 %reduce-scatter.2.cloned.1.call-done = f32[128,16,128]{2,1,0:T(8,128)} async-done(((f32[512,16,128]{2,1,0:T(8,128)}), f32[128,16,128]{2,1,0:T(8,128)}) %reduce-scatter.2.cloned.1.call-update) | async-done | bytes 1048592 | tf_op jit(solution)/shard_map/reduce_scatter | solution.py:276
  (1 shorter events, 0.0 us)
Async XLA Ops:
  6.5 38.9 %all-gather.2.cloned.1.call-start = ((), (), s32[]{:S(2)}) async-start(), calls=%async_computation.3 | async-start | bytes 5242880 | tf_op jit(solution)/shard_map/all_gather | solution.py:251
  11.1 11.9 %all-to-all-start = ((s32[1,32,2]{2,0,1:T(1,128)}), s32[1,32,2]{2,0,1:T(1,128)S(1)}, u32[]{:S(2)}, u32[]{:S(2)}) async-start(s32[1,32,2]{2,0,1:T(1,128)} %bitcast.8), calls=%async_computation | async-start | bytes 32768 | tf_op jit(solution)/shard_map/all_to_all | solution.py:264
  23.0 11.4 %all-to-all-start.1 = ((f32[8,32,2]{0,2,1:T(2,128)}), f32[8,32,2]{0,2,1:T(2,128)S(1)}, u32[]{:S(2)}, u32[]{:S(2)}) async-start(f32[8,32,2]{0,2,1:T(2,128)} %bitcast.11), calls=%async_computation.1 | async-start | bytes 65536 | tf_op jit(solution)/shard_map/all_to_all | solution.py:263
  28.5 264.6 %reduce-scatter.2.cloned.1.call-start = ((), (), s32[]{:S(2)}) async-start(), calls=%async_computation.4 | async-start | bytes 5242880 | tf_op jit(solution)/shard_map/reduce_scatter | solution.py:276
  241.8 2.4 copy-start
Sparse Core Ops, SparseCore 0:
  8.9 36.4 all-gather.1
  245.8 47.1 reduce-scatter.1

commit v2 on v1

--- a/solution.py
+++ b/solution.py
@@ -14,6 +14,8 @@
 ROWS = 4
 CHUNKS = 2
 SLOTS = HALF + 2
+PIECES = 4
+GROUP = 8
 
 centre_coef = -2.5
 near_coef = 4.0 / 3.0
@@ -28,22 +30,29 @@
 
 
 def wave_kernel(
-    fwd_prev, fwd_now, adj_late, adj_last, speed_in, drive_in,
+    anchors, fwd_prev, fwd_now, adj_late, adj_last, speed_in, drive_in,
     out_ref,
-    field, halo, edge, speed, drive,
-    load_sem, send_sem, recv_sem,
+    field, halo, edge, model, drive, total, inbox, arrived,
+    load_sem, send_sem, recv_sem, move_send, move_recv,
 ):
     count = lax.axis_size("slab")
     me = lax.axis_index("slab")
     shot = lax.axis_index("shot")
-    rows, cells, depth = speed.shape
+    rows, cells, depth = drive.shape
+    block = out_ref.shape[0]
+    piece = block // PIECES
     part = rows // CHUNKS
+    core_index = shot % 2
+    partner = shot + 1 - 2 * core_index
+    across = (shot + 2) % 4
+    beyond = (partner + 2) % 4
+    anchor = anchors[shot]
 
     loads = [
         pltpu.make_async_copy(fwd_now, field.at[0, 1, pl.ds(2, rows)], load_sem.at[0]),
         pltpu.make_async_copy(adj_last, field.at[1, 1, pl.ds(2, rows)], load_sem.at[1]),
         pltpu.make_async_copy(fwd_prev, field.at[0, 0, pl.ds(2, rows)], load_sem.at[2]),
-        pltpu.make_async_copy(speed_in, speed, load_sem.at[3]),
+        pltpu.make_async_copy(speed_in, model.at[pl.ds(shot * block, block)], load_sem.at[3]),
         pltpu.make_async_copy(adj_late, field.at[1, 0, pl.ds(2, rows)], load_sem.at[4]),
         pltpu.make_async_copy(drive_in, drive, load_sem.at[5]),
     ]
@@ -60,7 +69,12 @@
     def _():
         pl.semaphore_signal(barrier, inc=1, device_id=(shot, me + 1), device_id_type=MESH)
 
+    for other in (partner, across):
+        pl.semaphore_signal(barrier, inc=1, device_id=(other, me), device_id_type=MESH)
+
     border = jnp.zeros((2, cells, depth), jnp.float32)
+    total[0:GROUP] = jnp.zeros((GROUP, cells, depth), jnp.float32)
+    total[rows + GROUP : rows + 2 * GROUP] = jnp.zeros((GROUP, cells, depth), jnp.float32)
     for which in range(2):
         for slot in range(SLOTS):
             field[which, slot, 0:2] = border
@@ -86,7 +100,7 @@
         clear(1)
 
     peers = (me + count - 1) // count + (2 * count - 2 - me) // count
-    pl.semaphore_wait(barrier, peers)
+    pl.semaphore_wait(barrier, peers + 2)
 
     def transfer(which, step, side, chunk):
         span = pl.ds(chunk * part, part)
@@ -117,6 +131,31 @@
         def _():
             transfer(which, step, 0, chunk).wait_recv()
 
+    def move(kind, p, source, target, device):
+        return pltpu.make_async_remote_copy(
+            src_ref=source,
+            dst_ref=target,
+            send_sem=move_send.at[kind, p],
+            recv_sem=move_recv.at[kind, p],
+            device_id=(device, me),
+            device_id_type=MESH,
+        )
+
+    def model_across(p):
+        span = model.at[pl.ds(shot * block + p * piece, piece)]
+        return move(0, p, speed_in.at[pl.ds(p * piece, piece)], span, across)
+
+    def model_partner(p):
+        span = model.at[pl.ds(shot * block + p * piece, piece)]
+        return move(1, p, speed_in.at[pl.ds(p * piece, piece)], span, partner)
+
+    def model_onward(p):
+        span = model.at[pl.ds(across * block + p * piece, piece)]
+        return move(2, p, span, span, partner)
+
+    for p in range(PIECES):
+        model_across(p).start()
+
     for which in range(2):
         loads[which].wait()
         for chunk in range(CHUNKS):
@@ -130,8 +169,16 @@
             lax.fori_loop(0, part // 8, pack, 0)
             send(which, 0, chunk)
 
+    for p in range(PIECES):
+        model_partner(p).start()
     for load in loads[2:]:
         load.wait()
+    for p in range(PIECES):
+        model_across(p).wait_recv()
+        model_onward(p).start()
+    for p in range(PIECES):
+        model_partner(p).wait_recv()
+        model_onward(p).wait_recv()
 
     lane = lax.broadcasted_iota(jnp.int32, (ROWS, cells, depth), 2)
 
@@ -163,16 +210,16 @@
                     shift = (RDEPTH - NSTEP + k + depth) % depth
                     lap = lap + jnp.where(lane == RDEPTH, pltpu.roll(samples, shift, 2), 0.0)
                 older_cell = field[which, older, pl.ds(y + 2, ROWS)]
-                value = 2.0 * core - older_cell + speed[pl.ds(y, ROWS)] * lap
+                value = 2.0 * core - older_cell + model[pl.ds(anchor + y, ROWS)] * lap
                 if image:
                     if which == 0:
                         other = field[1, slot_of(NSTEP + 1 - k), pl.ds(y + 2, ROWS)]
                     else:
                         other = field[0, slot_of(NSTEP + 1 - k), pl.ds(y + 2, ROWS)]
                     if image == "first" and which == 0:
-                        out_ref[pl.ds(y, ROWS)] = value * other
+                        total[pl.ds(y + GROUP, ROWS)] = value * other
                     else:
-                        out_ref[pl.ds(y, ROWS)] = out_ref[pl.ds(y, ROWS)] + value * other
+                        total[pl.ds(y + GROUP, ROWS)] += value * other
                 if not last:
                     field[which, target, pl.ds(y + 2, ROWS)] = value
                     edge[which, k, 0, pl.ds(y, ROWS)] = value[:, 0:2]
@@ -200,6 +247,75 @@
     lax.fori_loop(HALF + 2, NSTEP, later, 0)
     advance(0, NSTEP, "more", True)
     advance(1, NSTEP, "more", True)
+
+    for p in range(PIECES):
+        model_across(p).wait_send()
+        model_partner(p).wait_send()
+        model_onward(p).wait_send()
+
+    def share(owner, start):
+        first = jnp.clip(owner * block + start - anchor, -GROUP, rows) + GROUP
+        return total[pl.ds(first, GROUP)]
+
+    def per_group(p, body):
+        def run(i, carry):
+            body(p * piece + i * GROUP)
+            return carry
+
+        lax.fori_loop(0, piece // GROUP, run, 0)
+
+    def pair_copy(kind, p):
+        return move(
+            3 + kind, p,
+            model.at[pl.ds(kind * block + p * piece, piece)],
+            inbox.at[kind, pl.ds(p * piece, piece)],
+            partner,
+        )
+
+    def far_copy(p):
+        return move(
+            5, p,
+            model.at[pl.ds(2 * block + p * piece, piece)],
+            arrived.at[pl.ds(p * piece, piece)],
+            across,
+        )
+
+    for kind, owner in ((0, beyond), (1, partner)):
+        for p in range(PIECES):
+            def fill(y):
+                model[pl.ds(kind * block + y, GROUP)] = share(owner, y)
+
+            per_group(p, fill)
+            pair_copy(kind, p).start()
+        if kind == 0:
+            for p in range(PIECES):
+                pair_copy(0, p).wait_recv()
+
+                def combine(y):
+                    model[pl.ds(2 * block + y, GROUP)] = (
+                        share(across, y) + inbox[0, pl.ds(y, GROUP)]
+                    )
+
+                per_group(p, combine)
+                far_copy(p).start()
+    for p in range(PIECES):
+        pair_copy(1, p).wait_recv()
+
+        def own(y):
+            out_ref[pl.ds(y, GROUP)] = share(shot, y) + inbox[1, pl.ds(y, GROUP)]
+
+        per_group(p, own)
+    for p in range(PIECES):
+        far_copy(p).wait_recv()
+
+        def finish(y):
+            out_ref[pl.ds(y, GROUP)] += arrived[pl.ds(y, GROUP)]
+
+        per_group(p, finish)
+    for p in range(PIECES):
+        pair_copy(0, p).wait_send()
+        pair_copy(1, p).wait_send()
+        far_copy(p).wait_send()
 
     def settle(step, carry):
         for which in range(2):
@@ -217,29 +333,36 @@
     lax.fori_loop(0, NSTEP, settle, 0)
 
 
-def waves(prev, now, late, last, speed, drive):
+def waves(anchors, prev, now, late, last, speed_model, drive):
     rows, cells, depth = now.shape
+    block = speed_model.shape[0]
+    model_rows = block * lax.axis_size("shot")
     anywhere = pl.BlockSpec(memory_space=pl.ANY)
     return pl.pallas_call(
         wave_kernel,
-        out_shape=jax.ShapeDtypeStruct((rows, cells, depth), jnp.float32),
-        in_specs=[anywhere] * 6,
+        out_shape=jax.ShapeDtypeStruct((block, cells, depth), jnp.float32),
+        in_specs=[pl.BlockSpec(memory_space=pltpu.SMEM)] + [anywhere] * 6,
         out_specs=pl.BlockSpec(memory_space=pltpu.VMEM),
         scratch_shapes=[
             pltpu.VMEM((2, SLOTS, rows + 4, cells, depth), jnp.float32),
             pltpu.VMEM((2, NSTEP, 2, rows, 2, depth), jnp.float32),
             pltpu.VMEM((2, NSTEP, 2, rows, 2, depth), jnp.float32),
+            pltpu.VMEM((model_rows, cells, depth), jnp.float32),
             pltpu.VMEM((rows, cells, depth), jnp.float32),
-            pltpu.VMEM((rows, cells, depth), jnp.float32),
+            pltpu.VMEM((rows + 2 * GROUP, cells, depth), jnp.float32),
+            pltpu.VMEM((2, block, cells, depth), jnp.float32),
+            pltpu.VMEM((block, cells, depth), jnp.float32),
             pltpu.SemaphoreType.DMA((6,)),
             pltpu.SemaphoreType.DMA((2, NSTEP, 2, CHUNKS)),
             pltpu.SemaphoreType.DMA((2, NSTEP, 2, CHUNKS)),
+            pltpu.SemaphoreType.DMA((6, PIECES)),
+            pltpu.SemaphoreType.DMA((6, PIECES)),
         ],
         compiler_params=pltpu.CompilerParams(
-            collective_id=0, has_side_effects=True, vmem_limit_bytes=60 * 1024 * 1024
+            collective_id=0, has_side_effects=True, vmem_limit_bytes=61 * 1024 * 1024
         ),
         name="waves",
-    )(prev, now, late, last, speed, drive)
+    )(anchors, prev, now, late, last, speed_model, drive)
 
 
 def per_device(fwd_prev, fwd_now, adj_late, adj_last, speed_model, anchors, traces, dest, rec_pos):
@@ -247,33 +370,20 @@
     late, last = (adj_late[0], adj_last[0])
     aper_rows, slab_cols, depth = now.shape
     device_count = lax.axis_size("shot") * lax.axis_size("slab")
-    anchor = lax.dynamic_index_in_dim(anchors, lax.axis_index("shot"), keepdims=False)
-    piece = lax.all_gather(speed_model, "shot", axis=0, tiled=True)
-    speed = lax.dynamic_slice_in_dim(piece, anchor, aper_rows, axis=0)
 
     target = dest[:, 0]
-    onehot = (target[:, None] == jnp.arange(device_count, dtype=jnp.int32)[None, :]).astype(
-        jnp.int32
-    )
-    rank = jnp.sum(onehot * (jnp.cumsum(onehot, axis=0) - 1), axis=1)
-    slot = target * CAP + rank
-    sample_buf = jnp.zeros((NSTEP, device_count * CAP), jnp.float32).at[:, slot].set(traces)
-    place_buf = jnp.zeros((1, device_count * CAP), jnp.int32).at[0, slot].set(rec_pos)
-    got_samples, got_places = (
-        lax.all_to_all(sample_buf, ("shot", "slab"), split_axis=1, concat_axis=1, tiled=True),
-        lax.all_to_all(place_buf, ("shot", "slab"), split_axis=1, concat_axis=1, tiled=True),
-    )
-    wide = jnp.pad(got_samples.T, ((0, 0), (0, depth - NSTEP)))
-    drive = jnp.zeros((aper_rows * slab_cols, depth), jnp.float32).at[got_places[0]].add(wide)
+    listed = target.shape[0]
+    index = jnp.arange(listed, dtype=jnp.int32)
+    ahead = (target[:, None] == target[None, :]) & (index[None, :] < index[:, None])
+    slot = target * CAP + jnp.sum(ahead.astype(jnp.int32), axis=1)
+    listing = jnp.concatenate([traces, rec_pos.astype(jnp.float32)[None, :]], axis=0)
+    sent = jnp.zeros((NSTEP + 1, device_count * CAP), jnp.float32).at[:, slot].set(listing)
+    got = lax.all_to_all(sent, ("shot", "slab"), split_axis=1, concat_axis=1, tiled=True)
+    places = got[NSTEP].astype(jnp.int32)
+    wide = jnp.pad(got[:NSTEP].T, ((0, 0), (0, depth - NSTEP)))
+    drive = jnp.zeros((aper_rows * slab_cols, depth), jnp.float32).at[places].add(wide)
     drive = drive.reshape(aper_rows, slab_cols, depth)
-
-    partial_value = waves(prev, now, late, last, speed, drive)
-
-    model_rows = speed_model.shape[0] * lax.axis_size("shot")
-    placed = lax.dynamic_update_slice_in_dim(
-        jnp.zeros((model_rows, slab_cols, depth), jnp.float32), partial_value, anchor, axis=0
-    )
-    return lax.psum_scatter(placed, "shot", scatter_dimension=0, tiled=True)
+    return waves(anchors, prev, now, late, last, speed_model, drive)
 
 
 def solution(mesh):

time: 302 us -> 251 us (0.83)
  waiting for transfers between devices: 61.7 us -> 0 us
  Pallas kernels: 193 us -> 229 us
  between operations: 15.4 us -> 0.03 us
  blocking collectives: 0 us -> 12 us
  starting transfers between devices: 11.9 us -> 0 us
  local copies, waits for them, and re-layouts: 12.3 us -> 3.14 us
    reduce_scatter x1 -> x0, waiting for transfers between devices: 47.3 us -> none  [per_device(): return lax.psum_scatter(placed, 'shot', scatter_dimension=0, tiled=True)]
    pallas_call x1, Pallas kernels: 193 us -> 229 us  [waves(): pl.pallas_call(wave_kernel, out_shape=jax.ShapeDtypeStruct((block, cells,...]
    all_to_all x0 -> x1, blocking collectives: none -> 12 us  [per_device(): lax.all_to_all(sent, ('shot', 'slab'), split_axis=1, concat_axis=1, tiled...]
    all_to_all x2 -> x0, starting transfers between devices: 11.9 us -> none  [the longest x1 6.36 us: per_device(): lax.all_to_all(place_buf, ('shot', 'slab'), split_axis=1, concat_axis=1,...]
    all_gather x1 -> x0, waiting for transfers between devices: 8.78 us -> none  [per_device(): piece = lax.all_gather(speed_model, 'shot', axis=0, tiled=True)]
    all_to_all x2 -> x0, waiting for transfers between devices: 4.86 us -> none  [the longest x1 4.53 us: per_device(): lax.all_to_all(sample_buf, ('shot', 'slab'), split_axis=1, concat_axis=1,...]
    dynamic_slice x2 -> x0, local copies, waits for them, and re-layouts: 4.3 us -> none  [the longest x1 3.05 us: per_device(): speed = lax.dynamic_slice_in_dim(piece, anchor, aper_rows, axis=0)]
  transfers between devices with their start and end apart: 4 -> 0, of which waited for: 4 -> 0; matrix products, arithmetic and copies ran while one was open for 3% -> 0% of each run, Pallas kernels for 0% -> 0%
where the time goes in v2:
time: 251 us; the launch traced here: 250 us
  Pallas kernels  229 us (91%)
  blocking collectives  12 us (5%)
  other arithmetic  5.92 us (2%)
  local copies, waits for them, and re-layouts  3.14 us (1%)
    pallas_call x1, Pallas kernels, waves(): pl.pallas_call(wave_kernel, out_shape=jax.ShapeDtypeStruct((block, cells,...  229 us
    all_to_all x1, blocking collectives, per_device(): lax.all_to_all(sent, ('shot', 'slab'), split_axis=1, concat_axis=1, tiled...  12 us

profile of v2, /device:TPU:9, one launch (start us, length us, event | category | flops | bytes accessed | tf_op | source)
XLA Modules:
  0.0 250.4 jit_solution(5111170387524830629)
XLA Ops:
  0.0 0.7 convert_bitcast_fusion
  0.7 0.9 convert_reduce_fusion
  1.6 0.7 fusion.7
  2.2 0.7 maximum_bitcast_fusion
  2.9 0.1 copy.14
  3.0 0.7 scatter_custom_fusion
  3.7 12.0 %all_to_all.9 = f32[9,32,2]{0,2,1:T(2,128)S(1)} all-to-all(f32[9,32,2]{0,2,1:T(2,128)S(1)} %bitcast.30), channel_id=1, replica_groups=mesh['shot'=4,'slab'=8] {'shot','slab'}, dimensions={1} | all-to-all | bytes 4608 | tf_op jit(solution)/shard_map/all_to_all | solution.py:381
  15.8 0.7 fusion.2
  16.4 0.1 convert_element_type.24
  16.6 2.3 scatter_custom_fusion.1
  18.9 229.3 %waves.1 = f32[128,16,128]{2,1,0:T(8,128)} custom-call(s32[4]{0:T(128)} %anchors.1, f32[256,16,128]{2,1,0:T(8,128)} %bitcast.25, f32[256,16,128]{2,1,0:T(8,128)} %bitcast.26, f32[256,16,128]{2,1,0:T(8,128)} %bitcast.27, f32[256,16,128]{2,1,0:T(8,128)} %bitcast.28, f32[128,16,128]{2,1,0:T(8,128)} %speed_in.1, f32[256,16,128]{2,1,0:T(8,128)} %bitcast.24), custom_call_target="tpu_custom_call" | custom-call | tf_op jit(solution)/shard_map/waves/pallas_call | solution.py:341
  248.2 2.3 copy.16
  (1 shorter events, 0.0 us)

commit v3 on v2

--- a/solution.py
+++ b/solution.py
@@ -30,10 +30,11 @@
 
 
 def wave_kernel(
-    anchors, fwd_prev, fwd_now, adj_late, adj_last, speed_in, drive_in,
+    anchors, fwd_prev, fwd_now, adj_late, adj_last, speed_in, packet,
     out_ref,
-    field, halo, edge, model, drive, total, inbox, arrived,
+    field, halo, edge, model, drive, total, inbox, arrived, gathered,
     load_sem, send_sem, recv_sem, move_send, move_recv,
+    slab_send, slab_recv, shot_send, shot_recv,
 ):
     count = lax.axis_size("slab")
     me = lax.axis_index("slab")
@@ -54,23 +55,27 @@
         pltpu.make_async_copy(fwd_prev, field.at[0, 0, pl.ds(2, rows)], load_sem.at[2]),
         pltpu.make_async_copy(speed_in, model.at[pl.ds(shot * block, block)], load_sem.at[3]),
         pltpu.make_async_copy(adj_late, field.at[1, 0, pl.ds(2, rows)], load_sem.at[4]),
-        pltpu.make_async_copy(drive_in, drive, load_sem.at[5]),
+        pltpu.make_async_copy(packet.at[me], gathered.at[shot, me], load_sem.at[5]),
     ]
     for load in loads:
         load.start()
 
     barrier = pltpu.get_barrier_semaphore()
 
-    @pl.when(me > 0)
-    def _():
-        pl.semaphore_signal(barrier, inc=1, device_id=(shot, me - 1), device_id_type=MESH)
-
-    @pl.when(me < count - 1)
-    def _():
-        pl.semaphore_signal(barrier, inc=1, device_id=(shot, me + 1), device_id_type=MESH)
-
-    for other in (partner, across):
+    shots = gathered.shape[0]
+
+    def greet_slab(offset, carry):
+        other = (me + offset) % count
+        pl.semaphore_signal(barrier, inc=1, device_id=(shot, other), device_id_type=MESH)
+        return carry
+
+    def greet_shot(offset, carry):
+        other = (shot + offset) % shots
         pl.semaphore_signal(barrier, inc=1, device_id=(other, me), device_id_type=MESH)
+        return carry
+
+    lax.fori_loop(1, count, greet_slab, 0)
+    lax.fori_loop(1, shots, greet_shot, 0)
 
     border = jnp.zeros((2, cells, depth), jnp.float32)
     total[0:GROUP] = jnp.zeros((GROUP, cells, depth), jnp.float32)
@@ -99,8 +104,41 @@
     def _():
         clear(1)
 
-    peers = (me + count - 1) // count + (2 * count - 2 - me) // count
-    pl.semaphore_wait(barrier, peers + 2)
+    pl.semaphore_wait(barrier, count + shots - 2)
+
+    def slab_copy(source, target):
+        return pltpu.make_async_remote_copy(
+            src_ref=packet.at[target],
+            dst_ref=gathered.at[shot, source],
+            send_sem=slab_send.at[target],
+            recv_sem=slab_recv.at[source],
+            device_id=(shot, target),
+            device_id_type=MESH,
+        )
+
+    def shot_copy(source, target):
+        return pltpu.make_async_remote_copy(
+            src_ref=gathered.at[source],
+            dst_ref=gathered.at[source],
+            send_sem=shot_send.at[target],
+            recv_sem=shot_recv.at[source],
+            device_id=(target, me),
+            device_id_type=MESH,
+        )
+
+    def over_slabs(act):
+        def run(offset, carry):
+            act((me + offset) % count)
+            return carry
+
+        lax.fori_loop(1, count, run, 0)
+
+    def over_shots(act):
+        def run(offset, carry):
+            act((shot + offset) % shots)
+            return carry
+
+        lax.fori_loop(1, shots, run, 0)
 
     def transfer(which, step, side, chunk):
         span = pl.ds(chunk * part, part)
@@ -155,6 +193,7 @@
 
     for p in range(PIECES):
         model_across(p).start()
+    over_slabs(lambda other: slab_copy(me, other).start())
 
     for which in range(2):
         loads[which].wait()
@@ -173,9 +212,35 @@
         model_partner(p).start()
     for load in loads[2:]:
         load.wait()
+    over_slabs(lambda other: slab_copy(other, other).wait_recv())
+    over_shots(lambda other: shot_copy(shot, other).start())
+
+    def build():
+        over_shots(lambda other: shot_copy(other, other).wait_recv())
+        listed = shots * count * gathered.shape[2]
+        samples = gathered[...].reshape(listed, depth)
+        row = lax.broadcasted_iota(jnp.int32, (1, listed), 1)
+        mine = (row % gathered.shape[2]) // CAP == shot
+        place = jnp.where(mine, samples.T[NSTEP : NSTEP + 1].astype(jnp.int32), -1)
+        band = 16 * cells
+        cell = lax.broadcasted_iota(jnp.int32, (band, listed), 0)
+
+        def fill(i, carry):
+            chosen = jnp.where(cell + i * band == place, 1.0, 0.0)
+            plane = jnp.dot(
+                chosen, samples,
+                precision=lax.Precision.HIGHEST, preferred_element_type=jnp.float32,
+            )
+            drive[pl.ds(i * 16, 16)] = plane.reshape(16, cells, depth)
+            return carry
+
+        lax.fori_loop(0, rows // 16, fill, 0)
+
     for p in range(PIECES):
         model_across(p).wait_recv()
         model_onward(p).start()
+        if p == 1:
+            build()
     for p in range(PIECES):
         model_partner(p).wait_recv()
         model_onward(p).wait_recv()
@@ -248,6 +313,8 @@
     advance(0, NSTEP, "more", True)
     advance(1, NSTEP, "more", True)
 
+    over_slabs(lambda other: slab_copy(me, other).wait_send())
+    over_shots(lambda other: shot_copy(shot, other).wait_send())
     for p in range(PIECES):
         model_across(p).wait_send()
         model_partner(p).wait_send()
@@ -333,7 +400,7 @@
     lax.fori_loop(0, NSTEP, settle, 0)
 
 
-def waves(anchors, prev, now, late, last, speed_model, drive):
+def waves(anchors, prev, now, late, last, speed_model, packet):
     rows, cells, depth = now.shape
     block = speed_model.shape[0]
     model_rows = block * lax.axis_size("shot")
@@ -352,38 +419,40 @@
             pltpu.VMEM((rows + 2 * GROUP, cells, depth), jnp.float32),
             pltpu.VMEM((2, block, cells, depth), jnp.float32),
             pltpu.VMEM((block, cells, depth), jnp.float32),
+            pltpu.VMEM((lax.axis_size("shot"),) + packet.shape, jnp.float32),
             pltpu.SemaphoreType.DMA((6,)),
             pltpu.SemaphoreType.DMA((2, NSTEP, 2, CHUNKS)),
             pltpu.SemaphoreType.DMA((2, NSTEP, 2, CHUNKS)),
             pltpu.SemaphoreType.DMA((6, PIECES)),
             pltpu.SemaphoreType.DMA((6, PIECES)),
+            pltpu.SemaphoreType.DMA((lax.axis_size("slab"),)),
+            pltpu.SemaphoreType.DMA((lax.axis_size("slab"),)),
+            pltpu.SemaphoreType.DMA((lax.axis_size("shot"),)),
+            pltpu.SemaphoreType.DMA((lax.axis_size("shot"),)),
         ],
         compiler_params=pltpu.CompilerParams(
             collective_id=0, has_side_effects=True, vmem_limit_bytes=61 * 1024 * 1024
         ),
         name="waves",
-    )(anchors, prev, now, late, last, speed_model, drive)
+    )(anchors, prev, now, late, last, speed_model, packet)
 
 
 def per_device(fwd_prev, fwd_now, adj_late, adj_last, speed_model, anchors, traces, dest, rec_pos):
     prev, now = (fwd_prev[0], fwd_now[0])
     late, last = (adj_late[0], adj_last[0])
-    aper_rows, slab_cols, depth = now.shape
-    device_count = lax.axis_size("shot") * lax.axis_size("slab")
+    depth = now.shape[2]
+    shots, slabs = lax.axis_size("shot"), lax.axis_size("slab")
 
     target = dest[:, 0]
-    listed = target.shape[0]
-    index = jnp.arange(listed, dtype=jnp.int32)
+    index = jnp.arange(target.shape[0], dtype=jnp.int32)
     ahead = (target[:, None] == target[None, :]) & (index[None, :] < index[:, None])
-    slot = target * CAP + jnp.sum(ahead.astype(jnp.int32), axis=1)
+    rank = jnp.sum(ahead.astype(jnp.int32), axis=1)
+    slot = ((target % slabs) * shots + target // slabs) * CAP + rank
     listing = jnp.concatenate([traces, rec_pos.astype(jnp.float32)[None, :]], axis=0)
-    sent = jnp.zeros((NSTEP + 1, device_count * CAP), jnp.float32).at[:, slot].set(listing)
-    got = lax.all_to_all(sent, ("shot", "slab"), split_axis=1, concat_axis=1, tiled=True)
-    places = got[NSTEP].astype(jnp.int32)
-    wide = jnp.pad(got[:NSTEP].T, ((0, 0), (0, depth - NSTEP)))
-    drive = jnp.zeros((aper_rows * slab_cols, depth), jnp.float32).at[places].add(wide)
-    drive = drive.reshape(aper_rows, slab_cols, depth)
-    return waves(anchors, prev, now, late, last, speed_model, drive)
+    wide = jnp.pad(listing.T, ((0, 0), (0, depth - NSTEP - 1)))
+    packet = jnp.zeros((slabs * shots * CAP, depth), jnp.float32).at[slot].set(wide)
+    packet = packet.reshape(slabs, shots * CAP, depth)
+    return waves(anchors, prev, now, late, last, speed_model, packet)
 
 
 def solution(mesh):

time: 251 us -> 247 us (0.984)
  blocking collectives: 12 us -> 0 us
  Pallas kernels: 229 us -> 240 us
  other arithmetic: 5.92 us -> 2.93 us
    all_to_all x1 -> x0, blocking collectives: 12 us -> none  [per_device(): lax.all_to_all(sent, ('shot', 'slab'), split_axis=1, concat_axis=1, tiled...]
    pallas_call x1, Pallas kernels: 229 us -> 240 us  [waves(): pl.pallas_call(wave_kernel, out_shape=jax.ShapeDtypeStruct((block, cells,...]
where the time goes in v3:
time: 247 us; the launch traced here: 246 us
  Pallas kernels  240 us (97%)
  local copies, waits for them, and re-layouts  3.59 us (1%)
  other arithmetic  2.93 us (1%)
    pallas_call x1, Pallas kernels, waves(): pl.pallas_call(wave_kernel, out_shape=jax.ShapeDtypeStruct((block, cells,...  240 us

profile of v3, /device:TPU:9, one launch (start us, length us, event | category | flops | bytes accessed | tf_op | source)
XLA Modules:
  0.0 246.5 jit_solution(6235660081504569897)
XLA Ops:
  0.0 0.7 convert_bitcast_fusion
  0.7 0.9 convert_reduce_fusion
  1.6 0.7 fusion.6
  2.2 0.7 maximum_bitcast_fusion
  2.9 0.1 copy.12
  3.0 1.2 scatter_custom_fusion
  4.3 239.9 %waves.1 = f32[128,16,128]{2,1,0:T(8,128)} custom-call(s32[4]{0:T(128)} %anchors.1, f32[256,16,128]{2,1,0:T(8,128)} %bitcast.17, f32[256,16,128]{2,1,0:T(8,128)} %bitcast.18, f32[256,16,128]{2,1,0:T(8,128)} %bitcast.19, f32[256,16,128]{2,1,0:T(8,128)} %bitcast.20, f32[128,16,128]{2,1,0:T(8,128)} %speed_in.1, f32[8,8,128]{2,1,0:T(8,128)} %bitcast.21), custom_call_target="tpu_custom_call" | custom-call | tf_op jit(solution)/shard_map/waves/pallas_call | solution.py:408
  244.2 2.3 copy.14

commit v4 on v3

--- a/solution.py
+++ b/solution.py
@@ -239,8 +239,6 @@
     for p in range(PIECES):
         model_across(p).wait_recv()
         model_onward(p).start()
-        if p == 1:
-            build()
     for p in range(PIECES):
         model_partner(p).wait_recv()
         model_onward(p).wait_recv()
@@ -300,7 +298,10 @@
         advance(1, k, None, False)
         return carry
 
-    lax.fori_loop(1, HALF + 1, early, 0)
+    advance(0, 1, None, False)
+    build()
+    advance(1, 1, None, False)
+    lax.fori_loop(2, HALF + 1, early, 0)
     advance(0, HALF + 1, "first", False)
     advance(1, HALF + 1, "first", False)
 

time: 247 us -> 240 us (0.972)
  Pallas kernels: 240 us -> 231 us
    pallas_call x1, Pallas kernels: 240 us -> 231 us  [waves(): pl.pallas_call(wave_kernel, out_shape=jax.ShapeDtypeStruct((block, cells,...]
where the time goes in v4:
time: 240 us; the launch traced here: 237 us
  Pallas kernels  231 us (96%)
  local copies, waits for them, and re-layouts  3.59 us (1%)
  other arithmetic  2.93 us (1%)
    pallas_call x1, Pallas kernels, waves(): pl.pallas_call(wave_kernel, out_shape=jax.ShapeDtypeStruct((block, cells,...  231 us

profile of v4, /device:TPU:9, one launch (start us, length us, event | category | flops | bytes accessed | tf_op | source)
XLA Modules:
  0.0 237.2 jit_solution(12603831561602847100)
XLA Ops:
  0.0 0.7 convert_bitcast_fusion
  0.7 0.9 convert_reduce_fusion
  1.6 0.7 fusion.6
  2.2 0.7 maximum_bitcast_fusion
  2.9 0.1 copy.12
  3.0 1.2 scatter_custom_fusion
  4.3 230.7 %waves.1 = f32[128,16,128]{2,1,0:T(8,128)} custom-call(s32[4]{0:T(128)} %anchors.1, f32[256,16,128]{2,1,0:T(8,128)} %bitcast.17, f32[256,16,128]{2,1,0:T(8,128)} %bitcast.18, f32[256,16,128]{2,1,0:T(8,128)} %bitcast.19, f32[256,16,128]{2,1,0:T(8,128)} %bitcast.20, f32[128,16,128]{2,1,0:T(8,128)} %speed_in.1, f32[8,8,128]{2,1,0:T(8,128)} %bitcast.21), custom_call_target="tpu_custom_call" | custom-call | tf_op jit(solution)/shard_map/waves/pallas_call | solution.py:409
  234.9 2.3 copy.14
